TPU v7x, 512 devices: a whole 4x8x8 slice. The times are simulated.
512 devices in a mesh: gx: 64 (over z, x, core), ta: 8 (over y).
Axes of the slice: x: 4, y: 8, z: 8, core: 2. Of those that a mesh axis runs over, the one named last changes fastest.
Arguments:
- d_out: bfloat16 [16384, 4096], P('gx', 'ta'), may hold values from -0.75 to 0.75
- kept: int32 [2048], P('gx'), may hold values from 0 to 16383, as said below
- expert_ids: int32 [2048, 8], P('gx'), may hold values from 0 to 63, all different within a row; in each aligned block of 32 rows (0 to 31, 32 to 63, ...) at most 8 rows name the same one
- gates: bfloat16 [2048, 8], P('gx'), may hold values from 0.049804688 to 1
- down_weight: bfloat16 [64, 1536, 4096], P('gx', 'ta'), may hold values from -0.15625 to 0.15625
- gate_pre: bfloat16 [64, 1536, 512], P('gx', 'ta'), may hold values from -6 to 6
- up_pre: bfloat16 [64, 1536, 512], P('gx', 'ta'), may hold values from -6 to 6
- query: bfloat16 [2048, 8192], P('gx', 'ta'), may hold values from -6 to 6
- keys: bfloat16 [2048, 512], P('gx'), may hold values from -6 to 6
- values: bfloat16 [2048, 512], P('gx'), may hold values from -6 to 6
- d_attn: bfloat16 [2048, 8192], P('gx', 'ta'), may hold values from -12 to 12
Outputs:
- d_down: bfloat16 [64, 1536, 4096], P('gx', 'ta')
- d_gate_pre: bfloat16 [64, 1536, 512], P('gx', 'ta')
- d_up_pre: bfloat16 [64, 1536, 512], P('gx', 'ta')
- d_gates: float32 [2048, 8], P('gx')
- d_query: bfloat16 [2048, 8192], P('gx', 'ta')
- d_key: float32 [2048, 512], P('gx')
- d_value: float32 [2048, 512], P('gx')
Inputs may be any that keep to these rules, and one draw needn't show every extreme that they name: `kept`: rising; the 32 selected tokens of block i lie in positions i * 256 to (i + 1) * 256 - 1 and include both ends. `expert_ids`: each row names 8 different experts; in each aligned block of 32 rows no expert is named more than 8 times.
All inputs are finite; a program needn't handle non-finite values.
Results may differ from a plain program's by a relative error of at most 0.0068.
Values may be sent and summed in bfloat16 or wider, within the bound.
No kernel may reach another device: no remote copies, remote signals or barrier semaphores. Data moves between devices by JAX's collectives and lax.ppermute only.
A program may use at most 64 MiB of HBM per device.

v0:
```python
import jax
import jax.numpy as jnp
from jax import lax
from jax.sharding import PartitionSpec as P

H = 64
KVH = 4
HD = 128


def on_device(
    d_out, kept, expert_ids, gates, down_weight, gate_pre, up_pre, query, keys, values, d_attn
):
    n_experts = lax.axis_size("gx")
    keep_dev = kept.shape[0]
    tok_dev = d_out.shape[0]
    top = expert_ids.shape[1]
    slot_count = gate_pre.shape[2]
    cap = slot_count // n_experts
    picked = jnp.take(d_out, kept % tok_dev, axis=0)
    flat_ids = expert_ids.reshape(-1)
    onehot = (flat_ids[:, None] == jnp.arange(n_experts, dtype=jnp.int32)[None, :]).astype(
        jnp.int32
    )
    rank = jnp.sum((jnp.cumsum(onehot, axis=0) - onehot) * onehot, axis=1)
    dest = flat_ids * cap + rank
    match = dest[:, None] == jnp.arange(slot_count, dtype=jnp.int32)[None, :]
    match_rows = jnp.sum(
        match.reshape(keep_dev, top, slot_count).astype(jnp.float32), axis=1
    ).astype(jnp.bfloat16)
    gate_slots = jnp.sum(jnp.where(match, gates.reshape(-1, 1).astype(jnp.float32), 0.0), axis=0)
    gate_slots = gate_slots.astype(jnp.bfloat16).reshape(n_experts, cap)
    full_rows = lax.all_gather(picked, "ta", axis=1, tiled=True)
    packed = lax.dot_general(
        match_rows, full_rows, (((0,), (0,)), ((), ())), preferred_element_type=jnp.float32
    )
    arrived = lax.all_to_all(
        packed.astype(jnp.bfloat16).reshape(n_experts, cap, full_rows.shape[1]),
        "gx",
        split_axis=0,
        concat_axis=0,
        tiled=True,
    )
    arrived_gates = lax.all_to_all(gate_slots, "gx", split_axis=0, concat_axis=0, tiled=True)
    slot_rows = arrived.reshape(slot_count, -1)
    slot_weight = arrived_gates.reshape(-1).astype(jnp.float32)
    weight = down_weight[0]
    z = lax.dot_general(
        weight, slot_rows, (((1,), (1,)), ((), ())), preferred_element_type=jnp.float32
    )
    g = gate_pre[0].astype(jnp.float32)
    u = up_pre[0].astype(jnp.float32)
    sig = jax.nn.sigmoid(g)
    act = g * sig
    hidden = act * u
    slot_dots = jnp.sum(hidden * z, axis=0)
    grad_hidden = z * slot_weight[None, :]
    grad_up = (grad_hidden * act).astype(jnp.bfloat16)[None]
    grad_gate = (grad_hidden * u * sig * (1.0 + g * (1.0 - sig))).astype(jnp.bfloat16)[None]
    weighted = (hidden * slot_weight[None, :]).astype(jnp.bfloat16)
    grad_weight = jnp.dot(weighted, slot_rows, preferred_element_type=jnp.float32).astype(
        jnp.bfloat16
    )[None]
    returned = lax.all_to_all(
        slot_dots.reshape(n_experts, cap), "gx", split_axis=0, concat_axis=0, tiled=True
    )
    gate_terms = jnp.sum(jnp.where(match, returned.reshape(1, -1), 0.0), axis=1).reshape(
        keep_dev, top
    )
    local_heads = query.shape[1] // HD
    group = H // KVH
    kv_local = max(1, local_heads // group)
    per_kv = local_heads // kv_local
    first_kv = lax.axis_index("ta") * local_heads // group
    key_local = lax.dynamic_slice_in_dim(keys, first_kv * HD, kv_local * HD, 1)
    value_local = lax.dynamic_slice_in_dim(values, first_kv * HD, kv_local * HD, 1)
    key_all, value_all = (
        lax.all_gather(key_local, "gx", axis=0, tiled=True),
        lax.all_gather(value_local, "gx", axis=0, tiled=True),
    )
    total = key_all.shape[0]
    key_three = key_all.reshape(total, kv_local, HD)
    value_three = value_all.reshape(total, kv_local, HD)
    query_four = query.reshape(keep_dev, kv_local, per_kv, HD)
    grad_four = d_attn.reshape(keep_dev, kv_local, per_kv, HD)
    scale = HD ** (-0.5)
    scores = (
        jnp.einsum("qcgd,kcd->cgqk", query_four, key_three, preferred_element_type=jnp.float32)
        * scale
    )
    query_pos = lax.axis_index("gx") * keep_dev + jnp.arange(keep_dev)
    causal = jnp.arange(total)[None, :] <= query_pos[:, None]
    scores = jnp.where(causal[None, None], scores, -1e30)
    top_score = jnp.max(scores, axis=3, keepdims=True)
    expo = jnp.exp(scores - top_score)
    probs = expo / jnp.sum(expo, axis=3, keepdims=True)
    grad_probs = jnp.einsum(
        "qcgd,kcd->cgqk", grad_four, value_three, preferred_element_type=jnp.float32
    )
    grad_scores = probs * (grad_probs - jnp.sum(probs * grad_probs, axis=3, keepdims=True))
    probs_b = probs.astype(jnp.bfloat16)
    grad_b = grad_scores.astype(jnp.bfloat16)
    grad_query = (
        jnp.einsum("cgqk,kcd->qcgd", grad_b, key_three, preferred_element_type=jnp.float32) * scale
    )
    grad_query = grad_query.astype(jnp.bfloat16).reshape(keep_dev, -1)
    key_part = (
        jnp.einsum("cgqk,qcgd->kcd", grad_b, query_four, preferred_element_type=jnp.float32) * scale
    )
    value_part = jnp.einsum(
        "cgqk,qcgd->kcd", probs_b, grad_four, preferred_element_type=jnp.float32
    )
    owned = lax.psum_scatter(
        jnp.concatenate(
            [
                key_part.reshape(keep_dev * lax.axis_size("gx"), -1),
                value_part.reshape(keep_dev * lax.axis_size("gx"), -1),
            ],
            axis=1,
        ),
        "gx",
        scatter_dimension=0,
        tiled=True,
    )
    width = kv_local * HD
    empty = jnp.zeros((keep_dev, KVH * HD), jnp.float32)
    key_full = lax.dynamic_update_slice(empty, owned[:, :width], (0, first_kv * HD))
    value_full = lax.dynamic_update_slice(empty, owned[:, width:], (0, first_kv * HD))
    grad_gates, grad_key, grad_value = lax.psum((gate_terms, key_full, value_full), "ta")
    return (grad_weight, grad_gate, grad_up, grad_gates, grad_query, grad_key, grad_value)


def solution(mesh):
    in_specs = (
        P("gx", "ta"),
        P("gx"),
        P("gx", None),
        P("gx", None),
        P("gx", "ta", None),
        P("gx", "ta", None),
        P("gx", "ta", None),
        P("gx", "ta"),
        P("gx", None),
        P("gx", None),
        P("gx", "ta"),
    )
    out_specs = (
        P("gx", "ta", None),
        P("gx", "ta", None),
        P("gx", "ta", None),
        P("gx", None),
        P("gx", "ta"),
        P("gx", None),
        P("gx", None),
    )
    return jax.shard_map(
        on_device, mesh=mesh, in_specs=in_specs, out_specs=out_specs, check_vma=False
    )
```

profile of v0, /device:TPU:2, one launch (start us, length us, event | category | flops | bytes accessed | tf_op | source)
XLA Modules:
  0.0 499.3 jit_solution(1224681247285578095)
XLA Ops:
  7.2 0.9 copy.53
  8.2 0.7 compare_and_fusion
  8.9 1.6 gather_fusion
  10.6 26.4 %all_gather.9 = bf16[32,4096]{1,0:T(8,128)(2,1)S(1)} all-gather(bf16[32,512]{1,0:T(8,128)(2,1)S(1)} %broadcast_select_fusion), channel_id=1, replica_groups=mesh['gx'=64,'ta'=8] {'ta'}, dimensions={1}, use_global_device_ids=true | all-gather | bytes 294912 | tf_op jit(solution)/shard_map/all_gather | solution.py:33
  37.0 0.6 reduce-window.6
  37.6 0.2 slice_reduce_fusion
  37.8 0.1 fusion.50
  38.1 0.2 convert_reduce_fusion
  38.3 3.2 fusion
  41.6 14.2 %all-to-all-start.1 = ((bf16[64,8,4096]{2,1,0:T(8,128)(2,1)}), bf16[64,8,4096]{2,1,0:T(8,128)(2,1)}, u32[]{:S(2)}, u32[]{:S(2)}) async-start(bf16[64,8,4096]{2,1,0:T(8,128)(2,1)} %fusion), calls=%async_computation.1 | async-start | bytes 8388608 | tf_op jit(solution)/shard_map/all_to_all | solution.py:37
  55.8 0.7 constant_dynamic-slice_fusion.1
  56.5 0.7 constant_dynamic-slice_fusion
  57.2 134.0 %all_gather.10 = bf16[2048,128]{1,0:T(8,128)(2,1)S(1)} all-gather(bf16[32,128]{1,0:T(8,128)(2,1)S(1)} %constant_dynamic-slice_fusion.1), channel_id=1, replica_groups=mesh['gx'=64,'ta'=8] {'gx'}, dimensions={0}, use_global_device_ids=true | all-gather | bytes 532480 | tf_op jit(solution)/shard_map/all_gather | solution.py:78
  191.3 48.7 %all_gather.11 = bf16[2048,128]{1,0:T(8,128)(2,1)S(1)} all-gather(bf16[32,128]{1,0:T(8,128)(2,1)S(1)} %constant_dynamic-slice_fusion), channel_id=1, replica_groups=mesh['gx'=64,'ta'=8] {'gx'}, dimensions={0}, use_global_device_ids=true | all-gather | bytes 532480 | tf_op jit(solution)/shard_map/all_gather | solution.py:79
  240.0 0.1 iota_compare_fusion.2
  240.1 0.5 fusion.64
  240.7 0.4 fusion.9
  241.1 0.4 copy-done.11
  241.5 0.6 multiply_reduce_fusion
  242.2 0.6 fusion.18
  242.8 0.4 fusion.7
  243.2 0.6 convolution_bitcast_fusion.1
  243.8 1.4 pad_maximum_fusion
  245.2 3.0 copy.68
  248.2 0.8 copy.56
  249.0 0.7 reshape.214
  249.7 0.4 fusion.17
  250.1 0.6 copy.98
  250.8 3.8 fusion.33
  254.6 0.7 all_to_all.15
  255.3 8.7 %all-to-all-start.2 = ((f32[64,1,8]{2,1,0:T(1,128)}), f32[64,1,8]{2,1,0:T(1,128)S(1)}, u32[]{:S(2)}, u32[]{:S(2)}) async-start(f32[64,1,8]{2,1,0:T(1,128)} %bitcast.11), calls=%async_computation.2 | async-start | bytes 65536 | tf_op jit(solution)/shard_map/all_to_all | solution.py:64
  264.0 132.1 %reduce-scatter.4.cloned.1.call-done = f32[32,256]{1,0:T(8,128)} async-done(((f32[2048,256]{1,0:T(8,128)}), f32[32,256]{1,0:T(8,128)}) %reduce-scatter.4.cloned.1.call-update) | async-done | bytes 32784
  396.1 0.7 slice_dynamic-update-slice_fusion.1
  396.9 0.5 broadcast.112
  397.4 0.7 reduce.12
  398.2 0.2 select_reduce_fusion
  398.5 0.7 convert_element_type.130
  399.2 8.1 %all-to-all-start = ((bf16[64,1,8]{2,1,0:T(2,128)(2,1)}), bf16[64,1,8]{2,1,0:T(2,128)(2,1)S(1)}, u32[]{:S(2)}, u32[]{:S(2)}) async-start(bf16[64,1,8]{2,1,0:T(2,128)(2,1)} %convert_element_type.130), calls=%async_computation | async-start | bytes 65536 | tf_op jit(solution)/shard_map/all_to_all | solution.py:44
  407.4 0.7 slice_dynamic-update-slice_fusion
  408.1 0.6 copy-done.2
  408.8 29.7 %psum.21 = f32[32,8]{1,0:T(8,128)S(1)} all-reduce(f32[32,8]{1,0:T(8,128)S(1)} %reshape.208), channel_id=1, replica_groups=mesh['gx'=64,'ta'=8] {'ta'}, use_global_device_ids=true, to_apply=%region_7.8 | all-reduce | flops 256 | bytes 2048 | tf_op jit(solution)/shard_map/psum | solution.py:129
  438.5 0.7 copy.67
  439.2 0.1 convert_reduce_fusion.1
  439.4 4.4 fusion.1
  443.8 0.9 fusion.43
  444.7 44.8 %all-reduce.3.cloned.1.call-done = (f32[32,512]{1,0:T(8,128)}, f32[32,512]{1,0:T(8,128)}) async-done(((f32[32,512]{1,0:T(8,128)}, f32[32,512]{1,0:T(8,128)}), (f32[32,512]{1,0:T(8,128)}, f32[32,512]{1,0:T(8,128)})) %all-reduce.3.cloned.1.call-update) | async-done | bytes 131088 | tf_op jit(solution)/shard_map/psum | solution.py:129
  489.5 1.5 copy.103
  491.0 1.5 copy.104
  (46 shorter events, 0.9 us)
Async XLA Ops:
  7.2 243.7 %copy-start = (bf16[1,192,4096]{2,1,0:T(8,128)(2,1)S(1)}, bf16[1,192,4096]{2,1,0:T(8,128)(2,1)}, u32[]{:S(2)}) copy-start(bf16[1,192,4096]{2,1,0:T(8,128)(2,1)} %param.15) | copy-start | bytes 4718596
  8.2 33.4 %copy-start.6 = (s32[256]{0:T(256)}, s32[256]{0:T(256)S(1)}, u32[]{:S(2)}) copy-start(s32[256]{0:T(256)S(1)} %reshape.204) | copy-start | bytes 3076
  38.0 3.6 copy-start.8
  41.6 198.6 %copy-start.1 = (bf16[32,1024]{1,0:T(8,128)(2,1)S(1)}, bf16[32,1024]{1,0:T(8,128)(2,1)}, u32[]{:S(2)}) copy-start(bf16[32,1024]{1,0:T(8,128)(2,1)} %param.18) | copy-start | bytes 196612
  41.6 209.3 %all-to-all-start.1 = ((bf16[64,8,4096]{2,1,0:T(8,128)(2,1)}), bf16[64,8,4096]{2,1,0:T(8,128)(2,1)}, u32[]{:S(2)}, u32[]{:S(2)}) async-start(bf16[64,8,4096]{2,1,0:T(8,128)(2,1)} %fusion), calls=%async_computation.1 | async-start | bytes 8388608 | tf_op jit(solution)/shard_map/all_to_all | solution.py:37
  55.8 340.4 %reduce-scatter.4.cloned.1.call-start = ((), (), s32[]{:S(2)}) async-start(), calls=%async_computation.4 | async-start | bytes 2129920
  240.7 0.8 copy-start.11
  248.2 2.7 copy-start.4
  248.2 2.7 copy-start.5
  249.7 1.1 copy-start.7
  249.7 1.1 copy-start.9
  250.8 147.4 %copy-start.10 = (f32[256]{0:T(256)S(1)}, f32[256]{0:T(256)}, u32[]{:S(2)}) copy-start(f32[256]{0:T(256)} %reshape.214) | copy-start | bytes 3076
  255.3 141.5 %all-to-all-start.2 = ((f32[64,1,8]{2,1,0:T(1,128)}), f32[64,1,8]{2,1,0:T(1,128)S(1)}, u32[]{:S(2)}, u32[]{:S(2)}) async-start(f32[64,1,8]{2,1,0:T(1,128)} %bitcast.11), calls=%async_computation.2 | async-start | bytes 65536 | tf_op jit(solution)/shard_map/all_to_all | solution.py:64
  396.8 11.2 %copy-start.3 = (f32[32,512]{1,0:T(8,128)}, f32[32,512]{1,0:T(8,128)S(1)}, u32[]{:S(2)}) copy-start(f32[32,512]{1,0:T(8,128)S(1)} %slice_dynamic-update-slice_fusion.1) | copy-start | bytes 196612
  399.2 40.0 %all-to-all-start = ((bf16[64,1,8]{2,1,0:T(2,128)(2,1)}), bf16[64,1,8]{2,1,0:T(2,128)(2,1)S(1)}, u32[]{:S(2)}, u32[]{:S(2)}) async-start(bf16[64,1,8]{2,1,0:T(2,128)(2,1)} %convert_element_type.130), calls=%async_computation | async-start | bytes 65536 | tf_op jit(solution)/shard_map/all_to_all | solution.py:44
  407.3 82.3 %all-reduce.3.cloned.1.call-start = ((), (), s32[]{:S(2)}) async-start(), calls=%async_computation.5 | async-start | bytes 262144 | tf_op jit(solution)/shard_map/psum | solution.py:129
  408.1 0.6 copy-start.2
Sparse Core Ops, SparseCore 0:
  248.3 147.7 reduce-scatter.3
  411.1 78.4 all-reduce.2
where the time goes:
time: 500 us; the launch traced here: 499 us
  blocking collectives  239 us (48%)
  waiting for transfers between devices  177 us (35%)
  starting transfers between devices  31 us (6%)
  local copies, waits for them, and re-layouts  17.8 us (4%)
  between operations  14.3 us (3%)
  matrix products  14 us (3%)
  other arithmetic  6.37 us (1%)
    all_gather x1, blocking collectives, on_device(): lax.all_gather(key_local, 'gx', axis=0, tiled=True)  134 us
    unnamed x3, waiting for transfers between devices  132 us
    all_gather x1, blocking collectives, on_device(): lax.all_gather(value_local, 'gx', axis=0, tiled=True)  48.7 us
    psum x1, waiting for transfers between devices, on_device(): lax.psum((gate_terms, key_full, value_full), 'ta')  44.8 us
    psum x1, blocking collectives, on_device(): lax.psum((gate_terms, key_full, value_full), 'ta')  29.7 us
    all_gather x1, blocking collectives, on_device(): full_rows = lax.all_gather(picked, 'ta', axis=1, tiled=True)  26.4 us
    all_to_all x1, starting transfers between devices, on_device(): lax.all_to_all(packed.astype(jnp.bfloat16).reshape(n_experts, cap, full_r...  14.2 us
  transfers between devices with their start and end apart: 5, of which 2 were waited for; matrix products, arithmetic and copies ran while one was open for 5% of the time, Pallas kernels for 0%

commit v1 on v0

--- a/solution.py
+++ b/solution.py
@@ -75,7 +75,9 @@
     key_local = lax.dynamic_slice_in_dim(keys, first_kv * HD, kv_local * HD, 1)
     value_local = lax.dynamic_slice_in_dim(values, first_kv * HD, kv_local * HD, 1)
     key_all, value_all = (
-        lax.all_gather(key_local, "gx", axis=0, tiled=True),
+        jnp.concatenate(
+            lax.all_to_all(jnp.stack([key_local] * lax.axis_size("gx")), "gx", 0, 0), axis=0
+        ),
         lax.all_gather(value_local, "gx", axis=0, tiled=True),
     )
     total = key_all.shape[0]

time: 500 us -> 462 us (0.924)
  blocking collectives: 239 us -> 191 us
  starting transfers between devices: 31 us -> 41.1 us
    all_gather x1 -> x0, blocking collectives: 134 us -> none  [on_device(): lax.all_gather(key_local, 'gx', axis=0, tiled=True)]
    all_gather x1, blocking collectives: 48.7 us -> 135 us  [on_device(): lax.all_gather(value_local, 'gx', axis=0, tiled=True)]
    all_to_all x0 -> x1, starting transfers between devices: none -> 13.9 us  [on_device(): lax.all_to_all(jnp.stack([key_local] * lax.axis_size('gx')), 'gx', 0, 0)]
  transfers between devices with their start and end apart: 5 -> 6, of which waited for: 2 -> 2; matrix products, arithmetic and copies ran while one was open for 5% -> 7% of each run, Pallas kernels for 0% -> 0%
where the time goes in v1:
time: 462 us; the launch traced here: 461 us
  blocking collectives  191 us (41%)
  waiting for transfers between devices  176 us (38%)
  starting transfers between devices  41.1 us (9%)
  local copies, waits for them, and re-layouts  17.7 us (4%)
  between operations  14.3 us (3%)
  matrix products  14 us (3%)
  other arithmetic  7.06 us (2%)
    all_gather x1, blocking collectives, on_device(): lax.all_gather(value_local, 'gx', axis=0, tiled=True)  135 us
    unnamed x3, waiting for transfers between devices  131 us
    psum x1, waiting for transfers between devices, on_device(): lax.psum((gate_terms, key_full, value_full), 'ta')  44.9 us
    psum x1, blocking collectives, on_device(): lax.psum((gate_terms, key_full, value_full), 'ta')  29.7 us
    all_gather x1, blocking collectives, on_device(): full_rows = lax.all_gather(picked, 'ta', axis=1, tiled=True)  26.4 us
    all_to_all x1, starting transfers between devices, on_device(): lax.all_to_all(jnp.stack([key_local] * lax.axis_size('gx')), 'gx', 0, 0)  13.9 us
    all_to_all x1, starting transfers between devices, on_device(): lax.all_to_all(packed.astype(jnp.bfloat16).reshape(n_experts, cap, full_r...  10.5 us
  transfers between devices with their start and end apart: 6, of which 2 were waited for; matrix products, arithmetic and copies ran while one was open for 7% of the time, Pallas kernels for 0%

profile of v1, /device:TPU:2, one launch (start us, length us, event | category | flops | bytes accessed | tf_op | source)
XLA Modules:
  0.0 461.1 jit_solution(15133598699042790482)
XLA Ops:
  7.2 0.8 constant_dynamic-slice_fusion.1
  8.1 0.9 stack.2
  8.9 13.9 %all-to-all-start.3 = ((bf16[64,32,128]{2,1,0:T(8,128)(2,1)}), bf16[64,32,128]{2,1,0:T(8,128)(2,1)S(1)}, u32[]{:S(2)}, u32[]{:S(2)}) async-start(bf16[64,32,128]{2,1,0:T(8,128)(2,1)} %stack.2), calls=%async_computation.3 | async-start | bytes 1048576 | tf_op jit(solution)/shard_map/all_to_all | solution.py:79
  22.8 0.8 copy.53
  23.7 0.7 compare_and_fusion
  24.4 0.6 reduce-window.6
  25.0 0.2 slice_reduce_fusion
  25.3 0.1 fusion.48
  25.5 0.6 gather_fusion
  26.2 26.4 %all_gather.6 = bf16[32,4096]{1,0:T(8,128)(2,1)S(1)} all-gather(bf16[32,512]{1,0:T(8,128)(2,1)S(1)} %broadcast_select_fusion), channel_id=1, replica_groups=mesh['gx'=64,'ta'=8] {'ta'}, dimensions={1}, use_global_device_ids=true | all-gather | bytes 294912 | tf_op jit(solution)/shard_map/all_gather | solution.py:33
  52.7 0.2 convert_reduce_fusion
  52.9 3.2 fusion
  56.2 10.5 %all-to-all-start.1 = ((bf16[64,8,4096]{2,1,0:T(8,128)(2,1)}), bf16[64,8,4096]{2,1,0:T(8,128)(2,1)}, u32[]{:S(2)}, u32[]{:S(2)}) async-start(bf16[64,8,4096]{2,1,0:T(8,128)(2,1)} %fusion), calls=%async_computation.1 | async-start | bytes 8388608 | tf_op jit(solution)/shard_map/all_to_all | solution.py:37
  66.8 0.7 constant_dynamic-slice_fusion
  67.5 134.8 %all_gather.7 = bf16[2048,128]{1,0:T(8,128)(2,1)S(1)} all-gather(bf16[32,128]{1,0:T(8,128)(2,1)S(1)} %constant_dynamic-slice_fusion), channel_id=1, replica_groups=mesh['gx'=64,'ta'=8] {'gx'}, dimensions={0}, use_global_device_ids=true | all-gather | bytes 532480 | tf_op jit(solution)/shard_map/all_gather | solution.py:81
  202.4 0.5 fusion.62
  202.9 0.4 fusion.9
  203.4 0.4 copy-done.10
  203.8 0.7 multiply_reduce_fusion
  204.4 0.6 fusion.18
  205.0 0.4 fusion.7
  205.4 0.6 convolution_bitcast_fusion.1
  206.0 1.4 pad_maximum_fusion
  207.4 3.0 copy.68
  210.4 0.8 copy.56
  211.2 0.7 reshape.218
  211.9 0.7 multiply_add_fusion.1
  212.6 0.4 fusion.17
  213.1 0.6 copy.98
  213.7 3.8 fusion.31
  217.5 0.7 all_to_all.18
  218.2 8.5 %all-to-all-start.2 = ((f32[64,1,8]{2,1,0:T(1,128)}), f32[64,1,8]{2,1,0:T(1,128)S(1)}, u32[]{:S(2)}, u32[]{:S(2)}) async-start(f32[64,1,8]{2,1,0:T(1,128)} %bitcast.11), calls=%async_computation.2 | async-start | bytes 65536 | tf_op jit(solution)/shard_map/all_to_all | solution.py:64
  226.7 131.1 %reduce-scatter.4.cloned.1.call-done = f32[32,256]{1,0:T(8,128)} async-done(((f32[2048,256]{1,0:T(8,128)}), f32[32,256]{1,0:T(8,128)}) %reduce-scatter.4.cloned.1.call-update) | async-done | bytes 32784
  357.8 0.7 slice_dynamic-update-slice_fusion.1
  358.6 0.5 broadcast.114
  359.1 0.7 reduce.12
  359.9 0.2 select_reduce_fusion
  360.2 0.7 convert_element_type.130
  360.9 8.1 %all-to-all-start = ((bf16[64,1,8]{2,1,0:T(2,128)(2,1)}), bf16[64,1,8]{2,1,0:T(2,128)(2,1)S(1)}, u32[]{:S(2)}, u32[]{:S(2)}) async-start(bf16[64,1,8]{2,1,0:T(2,128)(2,1)} %convert_element_type.130), calls=%async_computation | async-start | bytes 65536 | tf_op jit(solution)/shard_map/all_to_all | solution.py:44
  369.1 0.7 slice_dynamic-update-slice_fusion
  369.8 0.6 copy-done.3
  370.5 29.7 %psum.21 = f32[32,8]{1,0:T(8,128)S(1)} all-reduce(f32[32,8]{1,0:T(8,128)S(1)} %reshape.211), channel_id=1, replica_groups=mesh['gx'=64,'ta'=8] {'ta'}, use_global_device_ids=true, to_apply=%region_7.8 | all-reduce | flops 256 | bytes 2048 | tf_op jit(solution)/shard_map/psum | solution.py:131
  400.2 0.7 copy.67
  401.0 4.4 fusion.1
  405.4 0.9 fusion.41
  406.4 44.9 %all-reduce.3.cloned.1.call-done = (f32[32,512]{1,0:T(8,128)}, f32[32,512]{1,0:T(8,128)}) async-done(((f32[32,512]{1,0:T(8,128)}, f32[32,512]{1,0:T(8,128)}), (f32[32,512]{1,0:T(8,128)}, f32[32,512]{1,0:T(8,128)})) %all-reduce.3.cloned.1.call-update) | async-done | bytes 131088 | tf_op jit(solution)/shard_map/psum | solution.py:131
  451.3 1.5 copy.103
  452.8 1.5 copy.104
  (46 shorter events, 1.1 us)
Async XLA Ops:
  7.2 206.5 %copy-start = (bf16[1,192,4096]{2,1,0:T(8,128)(2,1)S(1)}, bf16[1,192,4096]{2,1,0:T(8,128)(2,1)}, u32[]{:S(2)}) copy-start(bf16[1,192,4096]{2,1,0:T(8,128)(2,1)} %param.15) | copy-start | bytes 4718596
  7.2 18.3 %copy-start.2 = (bf16[256,512]{1,0:T(8,128)(2,1)S(1)}, bf16[256,512]{1,0:T(8,128)(2,1)}, u32[]{:S(2)}) copy-start(bf16[256,512]{1,0:T(8,128)(2,1)} %param.11) | copy-start | bytes 786436
  8.9 47.2 %all-to-all-start.3 = ((bf16[64,32,128]{2,1,0:T(8,128)(2,1)}), bf16[64,32,128]{2,1,0:T(8,128)(2,1)S(1)}, u32[]{:S(2)}, u32[]{:S(2)}) async-start(bf16[64,32,128]{2,1,0:T(8,128)(2,1)} %stack.2), calls=%async_computation.3 | async-start | bytes 1048576 | tf_op jit(solution)/shard_map/all_to_all | solution.py:79
  23.6 2.5 copy-start.7
  25.4 0.8 copy-start.8
  56.2 146.2 %copy-start.1 = (bf16[32,1024]{1,0:T(8,128)(2,1)S(1)}, bf16[32,1024]{1,0:T(8,128)(2,1)}, u32[]{:S(2)}) copy-start(bf16[32,1024]{1,0:T(8,128)(2,1)} %param.18) | copy-start | bytes 196612
  56.2 157.5 %all-to-all-start.1 = ((bf16[64,8,4096]{2,1,0:T(8,128)(2,1)}), bf16[64,8,4096]{2,1,0:T(8,128)(2,1)}, u32[]{:S(2)}, u32[]{:S(2)}) async-start(bf16[64,8,4096]{2,1,0:T(8,128)(2,1)} %fusion), calls=%async_computation.1 | async-start | bytes 8388608 | tf_op jit(solution)/shard_map/all_to_all | solution.py:37
  66.7 291.1 %reduce-scatter.4.cloned.1.call-start = ((), (), s32[]{:S(2)}) async-start(), calls=%async_computation.5 | async-start | bytes 2129920
  202.9 0.8 copy-start.10
  210.4 3.3 copy-start.5
  210.4 3.3 copy-start.6
  213.7 146.2 %copy-start.9 = (f32[256]{0:T(256)S(1)}, f32[256]{0:T(256)}, u32[]{:S(2)}) copy-start(f32[256]{0:T(256)} %reshape.218) | copy-start | bytes 3076
  218.2 140.4 %all-to-all-start.2 = ((f32[64,1,8]{2,1,0:T(1,128)}), f32[64,1,8]{2,1,0:T(1,128)S(1)}, u32[]{:S(2)}, u32[]{:S(2)}) async-start(f32[64,1,8]{2,1,0:T(1,128)} %bitcast.11), calls=%async_computation.2 | async-start | bytes 65536 | tf_op jit(solution)/shard_map/all_to_all | solution.py:64
  358.6 11.2 %copy-start.4 = (f32[32,512]{1,0:T(8,128)}, f32[32,512]{1,0:T(8,128)S(1)}, u32[]{:S(2)}) copy-start(f32[32,512]{1,0:T(8,128)S(1)} %slice_dynamic-update-slice_fusion.1) | copy-start | bytes 196612
  360.9 40.0 %all-to-all-start = ((bf16[64,1,8]{2,1,0:T(2,128)(2,1)}), bf16[64,1,8]{2,1,0:T(2,128)(2,1)S(1)}, u32[]{:S(2)}, u32[]{:S(2)}) async-start(bf16[64,1,8]{2,1,0:T(2,128)(2,1)} %convert_element_type.130), calls=%async_computation | async-start | bytes 65536 | tf_op jit(solution)/shard_map/all_to_all | solution.py:44
  369.0 82.3 %all-reduce.3.cloned.1.call-start = ((), (), s32[]{:S(2)}) async-start(), calls=%async_computation.6 | async-start | bytes 262144 | tf_op jit(solution)/shard_map/psum | solution.py:131
  369.8 0.6 copy-start.3
Sparse Core Ops, SparseCore 0:
  210.5 147.2 reduce-scatter.3
  372.8 78.5 all-reduce.2
